TPU v7x, 32 devices: a whole 2x2x4 slice. The times are simulated.
32 devices in a mesh: py: 4 (over y, x), px: 8 (over z, core).
Axes of the slice: x: 2, y: 2, z: 4, core: 2. Of those that a mesh axis runs over, the one named last changes fastest.
Arguments:
- movie: bfloat16 [256, 128, 2048], P('py', 'px'), may hold values from -6 to 6
- traces: bfloat16 [4096, 2048], P('py', 'px'), may hold values from -0.125 to 0.125
- footprints: float32 [256, 128, 512], P('py', 'px'), may hold values from 0 to 1
- block_ids: int32 [4, 8, 4], P('py', 'px'), may hold values from 0 to 32, as said below
Outputs:
- updated: float32 [256, 128, 512], P('py', 'px')
Inputs may be any that keep to these rules, and one draw needn't show every extreme that they name: `block_ids`: in each tile's list of 4 entries the live entries come first and are distinct block numbers below 32; the remaining entries equal 32 and mark empty slots. Every tile has at least one live entry, and some tile has all 4 live.
All inputs are finite; a program needn't handle non-finite values.
Results may differ from a plain program's by a relative error of at most 0.0003.
Values may be sent and summed in bfloat16 or wider, within the bound.
A program may use at most 64 MiB of HBM per device.

v0:
```python
import jax
import jax.numpy as jnp
from jax import lax
from jax.sharding import PartitionSpec as P

K = 4096
BLK = 128
SLOTS = 4
ITERS = 2


def accumulate(tile_movie, picked):
    cross = lax.dot_general(
        tile_movie, picked, (((1,), (1,)), ((), ())), preferred_element_type=jnp.float32
    )
    gram = lax.dot_general(
        picked, picked, (((1,), (1,)), ((), ())), preferred_element_type=jnp.float32
    )
    return (cross, gram)


def per_device(movie, traces, footprints, block_ids):
    rows, cols, frames = movie.shape
    pixels = rows * cols
    width = SLOTS * BLK
    nblk = K // BLK
    tile_movie = movie.reshape(pixels, frames)
    ids = block_ids.reshape(SLOTS)
    onehot = (ids[:, None] == jnp.arange(nblk, dtype=jnp.int32)[None, :]).astype(jnp.float32)
    live = jnp.sum(onehot, axis=1)
    span_all = lax.all_gather(traces, "py", axis=0, tiled=True)
    span_len = span_all.shape[1]
    row_ids = lax.all_gather(block_ids, "px", axis=1, tiled=True).reshape(-1, SLOTS)
    route = (row_ids[:, :, None] == jnp.arange(nblk, dtype=jnp.int32)[None, None, :]).astype(
        jnp.bfloat16
    )
    outgoing = jnp.einsum(
        "rsb,bnw->rsnw",
        route,
        span_all.reshape(nblk, BLK, span_len),
        preferred_element_type=jnp.float32,
    )
    outgoing = outgoing.astype(jnp.bfloat16).reshape(row_ids.shape[0], width, span_len)
    received = lax.all_to_all(outgoing, "px", split_axis=0, concat_axis=2, tiled=True)
    mine = received.reshape(width, frames)
    cross, gram = accumulate(tile_movie, mine)
    column_live = jnp.repeat(live, BLK)
    denom = jnp.diagonal(gram) + 1e-06 + (1.0 - column_live)
    current = footprints.reshape(pixels, width) * column_live[None, :]
    pixall = pixels * lax.axis_size("py") * lax.axis_size("px")
    for step in range(ITERS):
        for slot in range(SLOTS):
            low = slot * BLK
            resid = cross[:, low : low + BLK] - jnp.dot(
                current, gram[:, low : low + BLK], precision=lax.Precision.HIGHEST
            )
            fresh = jnp.maximum(
                current[:, low : low + BLK] + resid / denom[None, low : low + BLK], 0.0
            )
            current = current.at[:, low : low + BLK].set(fresh)
        colsq = jnp.sum(current * current, axis=0).reshape(SLOTS, BLK)
        partial_value = jnp.einsum("sb,sn->bn", onehot, colsq, precision=lax.Precision.HIGHEST)
        totals = lax.psum(partial_value, ("py", "px"))
        factor = 1.0 / jnp.sqrt(totals / pixall + 1e-06)
        scale = jnp.einsum("sb,bn->sn", onehot, factor, precision=lax.Precision.HIGHEST).reshape(
            width
        )
        current = current * scale[None, :]
    return current.reshape(rows, cols, width)


def solution(mesh):
    return jax.shard_map(
        per_device,
        mesh=mesh,
        in_specs=(P("py", "px", None), P("py", "px"), P("py", "px", None), P("py", "px", None)),
        out_specs=P("py", "px", None),
        check_vma=False,
    )
```

profile of v0, /device:TPU:0, one launch (start us, length us, event | category | flops | bytes accessed | tf_op | source)
XLA Modules:
  0.0 233.0 jit_solution(12457084238456742489)
XLA Ops:
  6.5 0.0 all-gather.2.cloned.1.call-start
  6.5 0.7 all-gather.2.cloned.1.call-update
  7.3 13.6 %all_gather.6 = s32[1,8,4]{2,0,1:T(1,128)S(1)} all-gather(s32[1,1,4]{2,0,1:T(1,128)} %bitcast.62), channel_id=1, replica_groups=mesh['py'=4,'px'=8] {'px'}, dimensions={1}, use_global_device_ids=true | all-gather | bytes 144 | tf_op jit(solution)/shard_map/all_gather | solution.py:33
  20.9 0.1 copy.48
  21.0 26.1 %all-gather.2.cloned.1.call-done = bf16[4096,256]{1,0:T(8,128)(2,1)} async-done(((bf16[1024,256]{1,0:T(8,128)(2,1)}), bf16[4096,256]{1,0:T(8,128)(2,1)}) %all-gather.2.cloned.1.call-update) | async-done | bytes 2097168 | tf_op jit(solution)/shard_map/all_gather | solution.py:31
  47.1 2.9 %fusion.5 = bf16[8,4,128,256]{3,0,2,1:T(8,128)(2,1)S(1)} fusion(bf16[32,128,256]{2,1,0:T(8,128)(2,1)} %bitcast.60, s32[8,4]{0,1:T(4,128)S(1)} %bitcast.61), kind=kOutput, calls=%fused_computation.8 | convolution fusion | flops 68158464 | bytes 4194432 | tf_op jit(solution)/shard_map/rsb,bnw->rsnw/dot_general | solution.py:37
  50.0 1.7 copy.50
  51.7 0.0 copy-start.3
  51.8 4.7 %all-to-all-start = ((bf16[8,512,256]{2,1,0:T(8,128)(2,1)}), bf16[8,512,256]{2,1,0:T(8,128)(2,1)}, u32[]{:S(2)}, u32[]{:S(2)}) async-start(bf16[8,512,256]{2,1,0:T(8,128)(2,1)} %copy.50), calls=%async_computation | async-start | bytes 4194304 | tf_op jit(solution)/shard_map/all_to_all | solution.py:44
  56.5 0.0 copy-done.3
  56.5 0.0 copy-start.4
  56.5 1.8 copy.46
  58.3 0.6 compare_reduce_fusion.2
  59.0 0.7 compare_reduce_fusion
  59.7 0.0 copy-done.4
  59.7 0.2 convert_reduce_fusion
  59.9 0.1 broadcast_bitcast_fusion
  60.0 1.8 broadcast_multiply_fusion.2
  61.8 43.9 %all-to-all-done = bf16[8,512,256]{2,1,0:T(8,128)(2,1)} async-done(((bf16[8,512,256]{2,1,0:T(8,128)(2,1)}), bf16[8,512,256]{2,1,0:T(8,128)(2,1)}, u32[]{:S(2)}, u32[]{:S(2)}) %all-to-all-start) | async-done | bytes 2097184 | tf_op jit(solution)/shard_map/all_to_all | solution.py:44
  105.6 3.5 %fusion.8 = f32[512,512]{1,0:T(8,128)S(1)} fusion(bf16[8,512,256]{2,1,0:T(8,128)(2,1)} %all-to-all-done), kind=kOutput, calls=%fused_computation.10 | convolution fusion | flops 1073741824 | bytes 3145728 | tf_op jit(solution)/shard_map/dot_general | solution.py:16
  109.1 4.5 %gather_fusion = f32[512]{0:T(512)S(1)} fusion(f32[512,512]{1,0:T(8,128)S(1)} %fusion.8, s32[512]{0:T(512)S(1)} %bitcast.56), kind=kCustom, calls=%fused_computation | custom fusion | bytes 8192 | tf_op jit(solution)/shard_map/jit(diagonal)/cond/branch_0_fun/gather | solution.py:48
  113.7 0.1 subtract_add_fusion
  113.7 3.9 %copy.51 = bf16[1,512,8,256]{1,3,2,0:T(8,128)(2,1)} copy(bf16[1,512,8,256]{3,1,2,0:T(8,128)(2,1)} %bitcast.11) | data formatting | bytes 4194304 | tf_op jit(solution)/shard_map/all_to_all | solution.py:44
  117.7 5.2 %convolution_bitcast_fusion = f32[1024,512]{0,1:T(8,128)S(1)} fusion(bf16[512,2048]{0,1:T(8,128)(2,1)} %bitcast.59, bf16[1024,2048]{1,0:T(8,128)(2,1)} %bitcast.68), kind=kOutput, calls=%fused_computation.9 | convolution fusion | flops 2147483648 | bytes 8388608 | tf_op jit(solution)/shard_map/dot_general | solution.py:13
  122.9 0.0 copy-start.1
  122.9 2.1 fusion.40
  125.0 2.2 fusion.36
  127.2 2.1 fusion.32
  129.3 0.0 copy-done.1
  129.4 1.5 fusion.28
  130.9 0.2 multiply_reduce_fusion.1
  131.1 0.3 fusion.64
  131.3 37.2 %psum.14 = f32[32,128]{1,0:T(8,128)S(1)} all-reduce(f32[32,128]{1,0:T(8,128)S(1)} %fusion.64), channel_id=1, replica_groups=mesh['py'=4,'px'=8] {'py','px'}, use_global_device_ids=true, to_apply=%region_5.6 | all-reduce | flops 4096 | bytes 32768 | tf_op jit(solution)/shard_map/psum | solution.py:63
  168.5 0.2 convolution_bitcast_fusion.2
  168.7 0.0 copy-start.2
  168.7 0.2 broadcast_multiply_fusion.1
  168.9 1.4 copy-done.2
  170.3 2.1 fusion.25
  172.4 2.1 fusion.21
  174.6 2.0 fusion.17
  176.7 1.4 fusion.13
  178.1 0.0 copy-start
  178.2 1.3 copy-done
  179.5 0.2 multiply_reduce_fusion
  179.7 0.3 fusion.62
  179.9 42.4 %psum.15 = f32[32,128]{1,0:T(8,128)S(1)} all-reduce(f32[32,128]{1,0:T(8,128)S(1)} %fusion.62), channel_id=1, replica_groups=mesh['py'=4,'px'=8] {'py','px'}, use_global_device_ids=true, to_apply=%region_7.8 | all-reduce | flops 4096 | bytes 32768 | tf_op jit(solution)/shard_map/psum | solution.py:63
  222.3 0.2 convolution_bitcast_fusion.1
  222.5 1.8 broadcast_multiply_fusion
  224.3 1.8 copy.60
  (10 shorter events, 0.3 us)
Async XLA Ops:
  6.5 40.6 %all-gather.2.cloned.1.call-start = ((), (), s32[]{:S(2)}) async-start(), calls=%async_computation.1 | async-start | bytes 2621440 | tf_op jit(solution)/shard_map/all_gather | solution.py:31
  51.7 4.7 %copy-start.3 = (f32[64,16,512]{2,1,0:T(8,128)S(1)}, f32[64,16,512]{2,1,0:T(8,128)}, u32[]{:S(2)}) copy-start(f32[64,16,512]{2,1,0:T(8,128)} %param.22) | copy-start | bytes 6291460
  51.8 53.9 %all-to-all-start = ((bf16[8,512,256]{2,1,0:T(8,128)(2,1)}), bf16[8,512,256]{2,1,0:T(8,128)(2,1)}, u32[]{:S(2)}, u32[]{:S(2)}) async-start(bf16[8,512,256]{2,1,0:T(8,128)(2,1)} %copy.50), calls=%async_computation | async-start | bytes 4194304 | tf_op jit(solution)/shard_map/all_to_all | solution.py:44
  56.5 3.2 %copy-start.4 = (s32[1,1,4]{2,1,0:T(1,128)S(1)}, s32[1,1,4]{2,1,0:T(1,128)}, u32[]{:S(2)}) copy-start(s32[1,1,4]{2,1,0:T(1,128)} %param.23) | copy-start | bytes 52
  122.9 6.5 %copy-start.1 = (f32[1024,512]{0,1:T(8,128)}, f32[1024,512]{0,1:T(8,128)S(1)}, u32[]{:S(2)}) copy-start(f32[1024,512]{0,1:T(8,128)S(1)} %convolution_bitcast_fusion) | copy-start | bytes 6291460
  168.7 1.6 copy-start.2
  178.1 1.3 copy-start
Sparse Core Ops, SparseCore 0:
  9.2 37.8 all-gather.1
where the time goes:
time: 234 us; the launch traced here: 233 us
  blocking collectives  93.2 us (40%)
  waiting for transfers between devices  70.7 us (30%)
  matrix products  27.9 us (12%)
  local copies, waits for them, and re-layouts  17 us (7%)
  between operations  13.6 us (6%)
  other arithmetic  5.86 us (3%)
  starting transfers between devices  4.74 us (2%)
    psum x2, blocking collectives, per_device(): totals = lax.psum(partial_value, ('py', 'px'))  79.5 us
    all_to_all x1, waiting for transfers between devices, per_device(): lax.all_to_all(outgoing, 'px', split_axis=0, concat_axis=2, tiled=True)  43.9 us
    all_gather x1, waiting for transfers between devices, per_device(): span_all = lax.all_gather(traces, 'py', axis=0, tiled=True)  26.1 us
    dot_general x8, matrix products, per_device(): jnp.dot(current, gram[:, low:low + BLK], precision=lax.Precision.HIGHEST)  15.4 us
    all_gather x1, blocking collectives, per_device(): lax.all_gather(block_ids, 'px', axis=1, tiled=True).reshape(-1, SLOTS)  13.6 us
    dot_general x1, matrix products, accumulate(): lax.dot_general(tile_movie, picked, (((1,), (1,)), ((), ())), preferred_e...  5.2 us
    all_to_all x1, starting transfers between devices, per_device(): lax.all_to_all(outgoing, 'px', split_axis=0, concat_axis=2, tiled=True)  4.74 us
  transfers between devices with their start and end apart: 2, of which 2 were waited for; matrix products, arithmetic and copies ran while one was open for 2% of the time, Pallas kernels for 0%

commit v1 on v0

--- a/solution.py
+++ b/solution.py
@@ -41,7 +41,10 @@
         preferred_element_type=jnp.float32,
     )
     outgoing = outgoing.astype(jnp.bfloat16).reshape(row_ids.shape[0], width, span_len)
-    received = lax.all_to_all(outgoing, "px", split_axis=0, concat_axis=2, tiled=True)
+    received = jnp.concatenate(
+        lax.all_to_all(jnp.stack(jnp.split(outgoing, lax.axis_size("px"), axis=0)), "px", 0, 0),
+        axis=2,
+    )
     mine = received.reshape(width, frames)
     cross, gram = accumulate(tile_movie, mine)
     column_live = jnp.repeat(live, BLK)

time: 234 us -> 243 us (1.038)
  local copies, waits for them, and re-layouts: 17 us -> 26.2 us
    unnamed x10 -> x25, local copies, waits for them, and re-layouts: 2.71 us -> 8.13 us
    split x0 -> x1, local copies, waits for them, and re-layouts: none -> 4.79 us  [per_device(): jnp.split(outgoing, lax.axis_size('px'), axis=0)]
    all_to_all x1 -> x0, local copies, waits for them, and re-layouts: 3.92 us -> none  [per_device(): lax.all_to_all(outgoing, 'px', split_axis=0, concat_axis=2, tiled=True)]
where the time goes in v1:
time: 243 us; the launch traced here: 242 us
  blocking collectives  93.1 us (38%)
  waiting for transfers between devices  70.7 us (29%)
  matrix products  27.9 us (11%)
  local copies, waits for them, and re-layouts  26.2 us (11%)
  between operations  13.7 us (6%)
  other arithmetic  5.86 us (2%)
  starting transfers between devices  4.74 us (2%)
    psum x2, blocking collectives, per_device(): totals = lax.psum(partial_value, ('py', 'px'))  79.5 us
    all_to_all x1, waiting for transfers between devices, per_device(): lax.all_to_all(jnp.stack(jnp.split(outgoing, lax.axis_size('px'), axis=0)...  43.9 us
    all_gather x1, waiting for transfers between devices, per_device(): span_all = lax.all_gather(traces, 'py', axis=0, tiled=True)  26.1 us
    dot_general x8, matrix products, per_device(): jnp.dot(current, gram[:, low:low + BLK], precision=lax.Precision.HIGHEST)  15.4 us
    all_gather x1, blocking collectives, per_device(): lax.all_gather(block_ids, 'px', axis=1, tiled=True).reshape(-1, SLOTS)  13.6 us
    unnamed x25, local copies, waits for them, and re-layouts  8.13 us
    dot_general x1, matrix products, accumulate(): lax.dot_general(tile_movie, picked, (((1,), (1,)), ((), ())), preferred_e...  5.2 us
  transfers between devices with their start and end apart: 2, of which 2 were waited for; matrix products, arithmetic and copies ran while one was open for 2% of the time, Pallas kernels for 0%

profile of v1, /device:TPU:0, one launch (start us, length us, event | category | flops | bytes accessed | tf_op | source)
XLA Modules:
  0.0 242.2 jit_solution(6956425236938282568)
XLA Ops:
  6.5 0.0 all-gather.2.cloned.1.call-start
  6.5 0.7 all-gather.2.cloned.1.call-update
  7.3 13.6 %all_gather.6 = s32[1,8,4]{2,0,1:T(1,128)S(1)} all-gather(s32[1,1,4]{2,0,1:T(1,128)} %bitcast.76), channel_id=1, replica_groups=mesh['py'=4,'px'=8] {'px'}, dimensions={1}, use_global_device_ids=true | all-gather | bytes 144 | tf_op jit(solution)/shard_map/all_gather | solution.py:33
  20.9 0.1 copy.62
  21.0 26.1 %all-gather.2.cloned.1.call-done = bf16[4096,256]{1,0:T(8,128)(2,1)} async-done(((bf16[1024,256]{1,0:T(8,128)(2,1)}), bf16[4096,256]{1,0:T(8,128)(2,1)}) %all-gather.2.cloned.1.call-update) | async-done | bytes 2097168 | tf_op jit(solution)/shard_map/all_gather | solution.py:31
  47.1 2.9 %fusion.5 = bf16[8,4,128,256]{3,0,2,1:T(8,128)(2,1)S(1)} fusion(bf16[32,128,256]{2,1,0:T(8,128)(2,1)} %bitcast.66, s32[8,4]{0,1:T(4,128)S(1)} %bitcast.75), kind=kOutput, calls=%fused_computation.8 | convolution fusion | flops 68158464 | bytes 4194432 | tf_op jit(solution)/shard_map/rsb,bnw->rsnw/dot_general | solution.py:37
  50.0 4.8 %fusion.74 = (bf16[1,4,128,256]{3,0,2,1:T(2,128)(2,1)S(1)}, bf16[1,4,128,256]{3,0,2,1:T(2,128)(2,1)S(1)}, bf16[1,4,128,256]{3,0,2,1:T(2,128)(2,1)S(1)}, bf16[1,4...) fusion(bf16[8,4,128,256]{3,0,2,1:T(8,128)(2,1)S(1)} %fusion.5), kind=kLoop, calls=%fused_computation.112 | loop fusion | bytes 4194304 | tf_op jit(solution)/shard_map/split | solution.py:45
  54.9 0.7 constant_dynamic-update-slice_fusion.7
  56.0 0.7 constant_dynamic-update-slice_fusion.6
  56.7 0.7 constant_dynamic-update-slice_fusion.5
  57.4 0.7 constant_dynamic-update-slice_fusion.4
  58.1 0.7 constant_dynamic-update-slice_fusion.3
  58.9 0.7 constant_dynamic-update-slice_fusion.2
  59.6 0.7 constant_dynamic-update-slice_fusion.1
  60.3 0.7 constant_dynamic-update-slice_fusion
  61.0 0.0 copy-start.3
  61.0 4.7 %all-to-all-start = ((bf16[8,1,512,256]{3,2,1,0:T(8,128)(2,1)}), bf16[8,1,512,256]{3,2,1,0:T(8,128)(2,1)}, u32[]{:S(2)}, u32[]{:S(2)}) async-start(bf16[8,1,512,256]{3,2,1,0:T(8,128)(2,1)} %constant_dynamic-update-slice_fusion), calls=%async_computation | async-start | bytes 4194304 | tf_op jit(solution)/shard_map/all_to_all | solution.py:45
  65.8 0.0 copy-done.3
  65.8 0.0 copy-start.4
  65.8 1.8 copy.60
  67.6 0.6 compare_reduce_fusion.2
  68.3 0.7 compare_reduce_fusion
  69.0 0.0 copy-done.4
  69.0 0.2 convert_reduce_fusion
  69.2 0.1 broadcast_bitcast_fusion
  69.2 1.8 broadcast_multiply_fusion.2
  71.0 43.9 %all-to-all-done = bf16[8,1,512,256]{3,2,1,0:T(8,128)(2,1)} async-done(((bf16[8,1,512,256]{3,2,1,0:T(8,128)(2,1)}), bf16[8,1,512,256]{3,2,1,0:T(8,128)(2,1)}, u32[]{:S(2)}, u32[]{:S(2)}) %all-to-all-start) | async-done | bytes 2097184 | tf_op jit(solution)/shard_map/all_to_all | solution.py:45
  114.9 3.5 %fusion.8 = f32[512,512]{1,0:T(8,128)S(1)} fusion(bf16[8,1,512,256]{3,2,1,0:T(8,128)(2,1)} %all-to-all-done), kind=kOutput, calls=%fused_computation.10 | convolution fusion | flops 1073741824 | bytes 3145728 | tf_op jit(solution)/shard_map/dot_general | solution.py:16
  118.4 4.5 %gather_fusion = f32[512]{0:T(512)S(1)} fusion(f32[512,512]{1,0:T(8,128)S(1)} %fusion.8, s32[512]{0:T(512)S(1)} %bitcast.63), kind=kCustom, calls=%fused_computation | custom fusion | bytes 8192 | tf_op jit(solution)/shard_map/jit(diagonal)/cond/branch_0_fun/gather | solution.py:51
  122.9 0.1 subtract_add_fusion
  123.0 3.9 %copy.65 = bf16[1,512,8,256]{1,3,2,0:T(8,128)(2,1)} copy(bf16[1,512,8,256]{3,1,2,0:T(8,128)(2,1)} %bitcast.10) | data formatting | bytes 4194304 | tf_op jit(solution)/shard_map/reshape | solution.py:44
  126.9 5.2 %convolution_bitcast_fusion = f32[1024,512]{0,1:T(8,128)S(1)} fusion(bf16[512,2048]{0,1:T(8,128)(2,1)} %bitcast.65, bf16[1024,2048]{1,0:T(8,128)(2,1)} %bitcast.82), kind=kOutput, calls=%fused_computation.9 | convolution fusion | flops 2147483648 | bytes 8388608 | tf_op jit(solution)/shard_map/dot_general | solution.py:13
  132.2 0.0 copy-start.1
  132.2 2.1 fusion.40
  134.3 2.1 fusion.36
  136.5 2.1 fusion.32
  138.6 0.0 copy-done.1
  138.6 1.5 fusion.28
  140.1 0.2 multiply_reduce_fusion.1
  140.4 0.3 fusion.64
  140.6 37.1 %psum.14 = f32[32,128]{1,0:T(8,128)S(1)} all-reduce(f32[32,128]{1,0:T(8,128)S(1)} %fusion.64), channel_id=1, replica_groups=mesh['py'=4,'px'=8] {'py','px'}, use_global_device_ids=true, to_apply=%region_5.6 | all-reduce | flops 4096 | bytes 32768 | tf_op jit(solution)/shard_map/psum | solution.py:66
  177.8 0.2 convolution_bitcast_fusion.2
  177.9 0.0 copy-start.2
  177.9 0.2 broadcast_multiply_fusion.1
  178.2 1.4 copy-done.2
  179.6 2.1 fusion.25
  181.7 2.1 fusion.21
  183.8 2.0 fusion.17
  185.9 1.4 fusion.13
  187.4 0.0 copy-start
  187.4 1.3 copy-done
  188.7 0.2 multiply_reduce_fusion
  188.9 0.3 fusion.62
  189.2 42.4 %psum.15 = f32[32,128]{1,0:T(8,128)S(1)} all-reduce(f32[32,128]{1,0:T(8,128)S(1)} %fusion.62), channel_id=1, replica_groups=mesh['py'=4,'px'=8] {'py','px'}, use_global_device_ids=true, to_apply=%region_7.8 | all-reduce | flops 4096 | bytes 32768 | tf_op jit(solution)/shard_map/psum | solution.py:66
  231.6 0.2 convolution_bitcast_fusion.1
  231.8 1.8 broadcast_multiply_fusion
  233.6 1.8 copy.74
  (18 shorter events, 0.6 us)
Async XLA Ops:
  6.5 40.6 %all-gather.2.cloned.1.call-start = ((), (), s32[]{:S(2)}) async-start(), calls=%async_computation.1 | async-start | bytes 2621440 | tf_op jit(solution)/shard_map/all_gather | solution.py:31
  61.0 4.7 %copy-start.3 = (f32[64,16,512]{2,1,0:T(8,128)S(1)}, f32[64,16,512]{2,1,0:T(8,128)}, u32[]{:S(2)}) copy-start(f32[64,16,512]{2,1,0:T(8,128)} %param.22) | copy-start | bytes 6291460
  61.0 53.9 %all-to-all-start = ((bf16[8,1,512,256]{3,2,1,0:T(8,128)(2,1)}), bf16[8,1,512,256]{3,2,1,0:T(8,128)(2,1)}, u32[]{:S(2)}, u32[]{:S(2)}) async-start(bf16[8,1,512,256]{3,2,1,0:T(8,128)(2,1)} %constant_dynamic-update-slice_fusion), calls=%async_computation | async-start | bytes 4194304 | tf_op jit(solution)/shard_map/all_to_all | solution.py:45
  65.8 3.2 %copy-start.4 = (s32[1,1,4]{2,1,0:T(1,128)S(1)}, s32[1,1,4]{2,1,0:T(1,128)}, u32[]{:S(2)}) copy-start(s32[1,1,4]{2,1,0:T(1,128)} %param.23) | copy-start | bytes 52
  132.2 6.5 %copy-start.1 = (f32[1024,512]{0,1:T(8,128)}, f32[1024,512]{0,1:T(8,128)S(1)}, u32[]{:S(2)}) copy-start(f32[1024,512]{0,1:T(8,128)S(1)} %convolution_bitcast_fusion) | copy-start | bytes 6291460
  177.9 1.6 copy-start.2
  187.4 1.3 copy-start
Sparse Core Ops, SparseCore 0:
  9.2 37.8 all-gather.1
